TPU v7x, 256 devices: a whole 4x4x8 slice. The times are simulated.
256 devices in a mesh: group: 16 (over y, x), member: 16 (over z, core).
Axes of the slice: x: 4, y: 4, z: 8, core: 2. Of those that a mesh axis runs over, the one named last changes fastest.
Arguments:
- queries: bfloat16 [65536, 6144], P(('group', 'member')), may hold values from -64 to 64
- keys_values: bfloat16 [512, 128, 2048], P('group', 'member'), may hold values from -8 to 8
- local_lists: int32 [512, 5], P(('group', 'member')), may hold values from -1 to 31, as said below
- remote_lists: int32 [512, 3], P(('group', 'member')), may hold values from -1 to 15, as said below
- send_blocks: int32 [16, 16], P('group'), may hold values from 0 to 31
Outputs:
- attended: bfloat16 [65536, 6144], P(('group', 'member'))
Inputs may be any that keep to these rules, and one draw needn't show every extreme that they name: `local_lists`: row i lists distinct blocks of its slab, numbered 0 to 31 within the slab, then -1 in the remaining entries; the first entry is i mod 32, the row's own block. Some row lists 5 blocks. `remote_lists`: row i lists distinct slabs other than its own slab i // 32, then -1 in the remaining entries; a row may list none. Some row lists 3 slabs.
All inputs are finite; a program needn't handle non-finite values.
Results may differ from a plain program's by a relative error of at most 0.0038.
Values may be sent and summed in bfloat16 or wider, within the bound.
A program may use at most 128 MiB of HBM per device.

v0:
```python
import jax
import jax.numpy as jnp
from jax import lax
from jax.sharding import PartitionSpec as P

HEADS = 48
KV_HEADS = 8
HEAD_DIM = 128


def attend_rows(query_rows, listed, usable):
    block_rows = query_rows.shape[0]
    key_width = KV_HEADS * HEAD_DIM
    repeat = HEADS // KV_HEADS
    query_heads = query_rows.reshape(block_rows, KV_HEADS, repeat, HEAD_DIM)
    keys_all = listed[:, :, :key_width].reshape(
        listed.shape[0], listed.shape[1], KV_HEADS, HEAD_DIM
    )
    values_all = listed[:, :, key_width:].reshape(
        listed.shape[0], listed.shape[1], KV_HEADS, HEAD_DIM
    )
    halves = 2
    head_span = KV_HEADS // halves
    pieces = []
    for part_index in range(halves):
        start_head = part_index * head_span
        query_part = query_heads[:, start_head : start_head + head_span]
        keys_part = keys_all[:, :, start_head : start_head + head_span]
        values_part = values_all[:, :, start_head : start_head + head_span]
        scores = jnp.einsum(
            "qgrd,pkgd->qgrpk", query_part, keys_part, preferred_element_type=jnp.float32
        )
        scores = scores * HEAD_DIM ** (-0.5)
        scores = jnp.where(usable[:, None], scores, -jnp.inf)
        maxima = jnp.max(scores, axis=(3, 4), keepdims=True)
        weights = jnp.exp(scores - maxima)
        totals = jnp.sum(weights, axis=(3, 4))
        rounded = weights.astype(jnp.bfloat16)
        blended = jnp.einsum(
            "qgrpk,pkgd->qgrd", rounded, values_part, preferred_element_type=jnp.float32
        )
        pieces.append(blended / totals[..., None])
    joined = jnp.concatenate(pieces, axis=1)
    return joined.reshape(block_rows, HEADS * HEAD_DIM).astype(jnp.bfloat16)


def shards(queries, keys_values, local_lists, remote_lists, send_blocks):
    targets = send_blocks[0]
    query_count = local_lists.shape[0]
    block_rows = queries.shape[0] // query_count
    outputs = []
    outgoing = jnp.take(keys_values, targets, axis=0)
    arrived = lax.all_to_all(outgoing, "group", split_axis=0, concat_axis=0, tiled=True)
    group_pool = lax.all_gather(keys_values, "member", axis=1, tiled=True)
    cast_pool = lax.all_gather(arrived, "member", axis=1, tiled=True)
    for query_block in range(query_count):
        local_row = local_lists[query_block]
        remote_row = remote_lists[query_block]
        listed = jnp.concatenate(
            [
                jnp.take(group_pool, jnp.maximum(local_row, 0), axis=0),
                jnp.take(cast_pool, jnp.maximum(remote_row, 0), axis=0),
            ],
            axis=0,
        )
        usable = jnp.concatenate([local_row >= 0, remote_row >= 0])
        query_rows = queries[query_block * block_rows : (query_block + 1) * block_rows]
        outputs.append(attend_rows(query_rows, listed, usable))
    return jnp.concatenate(outputs, axis=0)


def solution(mesh):
    placed = (
        P(("group", "member"), None),
        P("group", "member", None),
        P(("group", "member"), None),
        P(("group", "member"), None),
        P("group", None),
    )
    return jax.shard_map(
        shards, mesh=mesh, in_specs=placed, out_specs=P(("group", "member"), None), check_vma=False
    )
```

profile of v0, /device:TPU:14, one launch (start us, length us, event | category | flops | bytes accessed | tf_op | source)
XLA Modules:
  0.0 305.4 jit_solution(815406715089342255)
XLA Ops:
  6.5 0.0 all-gather.5.cloned.1.call-start
  6.5 0.7 fusion.54
  7.2 0.7 compare_and_fusion.4
  7.9 1.8 gather_fusion
  9.7 0.1 broadcast_select_fusion.4
  9.8 15.2 %all_to_all.5 = bf16[16,8,2048]{2,1,0:T(8,128)(2,1)} all-to-all(bf16[16,8,2048]{2,1,0:T(8,128)(2,1)S(1)} %broadcast_select_fusion.4), channel_id=1, replica_groups=mesh['group'=16,'member'=16] {'group'}, dimensions={0} | all-to-all | bytes 1048576 | tf_op jit(solution)/shard_map/all_to_all | solution.py:53
  25.0 0.0 all-gather.5.cloned.1.call-update
  25.1 0.0 all-gather.3.cloned.1.call-start
  25.1 0.7 all-gather.3.cloned.1.call-update
  25.8 2.1 fusion.63
  27.9 0.0 copy-start.11
  27.9 0.0 copy-start.10
  27.9 1.6 copy.82
  29.5 1.6 copy.89
  31.1 0.0 copy-done.11
  31.1 0.0 copy-done.10
  31.1 0.1 pad_add_fusion
  31.3 51.9 %all-gather.5.cloned.1.call-done = bf16[16,128,2048]{2,1,0:T(8,128)(2,1)} async-done(((bf16[16,8,2048]{2,1,0:T(8,128)(2,1)}), bf16[16,128,2048]{2,1,0:T(8,128)(2,1)}) %all-gather.5.cloned.1.call-update) | async-done | bytes 8388624 | tf_op jit(solution)/shard_map/all_gather | solution.py:55
  83.2 4.0 %gather_fusion.4 = bf16[3,128,2048]{2,1,0:T(8,128)(2,1)S(1)} fusion(bf16[16,128,2048]{2,1,0:T(8,128)(2,1)} %all-gather.5.cloned.1.call-done, s32[1024]{0:T(1024)S(1)} %pad_clamp_fusion), kind=kCustom, calls=%fused_computation.3.clone | custom fusion | bytes 3145740 | tf_op jit(solution)/shard_map/jit(_take)/gather | solution.py:62
  87.3 4.0 %gather_fusion.2 = bf16[3,128,2048]{2,1,0:T(8,128)(2,1)S(1)} fusion(bf16[16,128,2048]{2,1,0:T(8,128)(2,1)} %all-gather.5.cloned.1.call-done, s32[1024]{0:T(1024)S(1)} %pad_clamp_fusion.2), kind=kCustom, calls=%fused_computation.1.clone | custom fusion | bytes 3145740 | tf_op jit(solution)/shard_map/jit(_take)/gather | solution.py:62
  91.3 2.0 broadcast_select_fusion.2
  93.3 85.7 %all-gather.3.cloned.1.call-done = bf16[32,128,2048]{2,1,0:T(8,128)(2,1)} async-done(((bf16[32,8,2048]{2,1,0:T(8,128)(2,1)}), bf16[32,128,2048]{2,1,0:T(8,128)(2,1)}) %all-gather.3.cloned.1.call-update) | async-done | bytes 16777232 | tf_op jit(solution)/shard_map/all_gather | solution.py:54
  179.0 8.1 %gather_fusion.3 = bf16[5,128,2048]{2,1,0:T(8,128)(2,1)} fusion(bf16[32,128,2048]{2,1,0:T(8,128)(2,1)} %all-gather.3.cloned.1.call-done, s32[1024]{0:T(1024)S(1)} %pad_clamp_fusion.1), kind=kCustom, calls=%fused_computation.2.clone | custom fusion | bytes 5242900 | tf_op jit(solution)/shard_map/jit(_take)/gather | solution.py:61
  187.1 8.1 %gather_fusion.1 = bf16[5,128,2048]{2,1,0:T(8,128)(2,1)} fusion(bf16[32,128,2048]{2,1,0:T(8,128)(2,1)} %all-gather.3.cloned.1.call-done, s32[1024]{0:T(1024)S(1)} %pad_clamp_fusion.4), kind=kCustom, calls=%fused_computation.clone | custom fusion | bytes 5242900 | tf_op jit(solution)/shard_map/jit(_take)/gather | solution.py:61
  195.3 3.2 %broadcast_select_fusion = (bf16[5,128,2048]{2,1,0:T(8,128)(2,1)S(1)}, bf16[5,128,2048]{2,1,0:T(8,128)(2,1)S(1)}) fusion(bf16[5,128,2048]{2,1,0:T(8,128)(2,1)} %gather_fusion.3, pred[5]{0:T(512)(128)(4,1)S(1)} %get-tuple-element.37, bf16[5,128,2048]{2,1,0:T(8,128)(2,1)} %gather_fusion.1, pred[5]{0:T(512)(128)(4,1)S(1)} %get-tuple-element.11), kind=kLoop, calls=%fused_computation.42 | loop fusion | flops 2621440 | bytes 10485770 | tf_op jit(solution)/shard_map/jit(_take)/select_n | solution.py:61
  198.5 0.0 copy-done
  198.5 2.3 fusion.24
  200.7 3.9 %copy.43 = bf16[8,128,1024]{1,2,0:T(8,128)(2,1)} copy(bf16[8,128,1024]{2,1,0:T(8,128)(2,1)} %get-tuple-element.21) | data formatting | bytes 4194304 | tf_op jit(solution)/shard_map/slice | solution.py:19
  204.6 3.1 %fusion.66 = (bf16[8,128,4,128]{1,3,2,0:T(8,128)(2,1)}, bf16[8,128,4,128]{1,3,2,0:T(8,128)(2,1)}) fusion(bf16[8,128,8,128]{1,3,2,0:T(8,128)(2,1)} %bitcast.206), kind=kLoop, calls=%fused_computation.115 | loop fusion | bytes 4194304 | tf_op jit(solution)/shard_map/slice | solution.py:29
  207.7 3.9 %copy.45 = bf16[8,128,1024]{1,2,0:T(8,128)(2,1)} copy(bf16[8,128,1024]{2,1,0:T(8,128)(2,1)} %get-tuple-element.22) | data formatting | bytes 4194304 | tf_op jit(solution)/shard_map/slice | solution.py:16
  211.6 3.1 %fusion.67 = (bf16[8,128,4,128]{1,3,2,0:T(8,128)(2,1)}, bf16[8,128,4,128]{1,3,2,0:T(8,128)(2,1)}) fusion(bf16[8,128,8,128]{1,3,2,0:T(8,128)(2,1)} %bitcast.207), kind=kLoop, calls=%fused_computation.116 | loop fusion | bytes 4194304 | tf_op jit(solution)/shard_map/slice | solution.py:28
  214.8 2.3 copy.88
  217.0 2.3 copy.92
  219.3 3.4 %fusion.25 = (bf16[8,128,1024]{2,1,0:T(8,128)(2,1)}, bf16[8,128,1024]{2,1,0:T(8,128)(2,1)}) fusion(bf16[5,128,2048]{2,1,0:T(8,128)(2,1)S(1)} %get-tuple-element.48, bf16[3,128,2048]{2,1,0:T(8,128)(2,1)} %get-tuple-element.50), kind=kLoop, calls=%fused_computation.45 | loop fusion | flops 8388608 | bytes 8388608 | tf_op jit(solution)/shard_map/concatenate | solution.py:59
  222.8 3.0 copy.32
  225.8 1.5 fusion.64
  227.3 3.0 copy.34
  230.3 0.0 copy-start.1
  230.3 1.5 fusion.65
  231.8 2.4 copy.81
  234.2 2.3 copy.85
  236.5 0.0 copy-done.1
  236.5 0.0 copy-done.3
  236.5 6.3 %bitcast_reduce_fusion.1 = (f32[128,4,6]{0,2,1:T(8,128)S(1)}, f32[4,8,128,128,6]{3,2,4,1,0:T(8,128)}) fusion(pred[8]{0:T(512)(128)(4,1)S(1)} %get-tuple-element.52, bf16[128,8,6,128]{0,3,2,1:T(8,128)(2,1)S(1)} %bitcast.214, bf16[8,128,4,128]{3,1,0,2:T(8,128)(2,1)S(1)} %copy-done.1), kind=kOutput, calls=%fused_computation.9 | convolution fusion | flops 814740480 | bytes 14430720 | tf_op jit(solution)/shard_map/qgrd,pkgd->qgrpk/dot_general | solution.py:30
  242.8 0.0 copy-done.5
  242.8 7.5 %fusion.8 = (f32[128,4,6]{0,2,1:T(8,128)S(1)}, f32[128,4,6]{0,2,1:T(8,128)S(1)}, f32[4,8,128,128,6]{3,2,4,1,0:T(8,128)S(1)}) fusion(f32[4,8,128,128,6]{3,2,4,1,0:T(8,128)} %get-tuple-element.42, f32[128,4,6]{0,2,1:T(8,128)S(1)} %get-tuple-element.41, pred[8]{0:T(512)(128)(4,1)S(1)} %get-tuple-element.52, bf16[128,8,6,128]{0,3,2,1:T(8,128)(2,1)S(1)} %bitcast.215, ...), kind=kOutput, calls=%fused_computation.25 | convolution fusion | flops 827320320 | bytes 27042304 | tf_op jit(solution)/shard_map/qgrd,pkgd->qgrpk/dot_general | solution.py:30
  250.3 0.0 copy-done.9
  250.3 7.6 %fusion.27 = bf16[128,4,6,128]{0,3,2,1:T(8,128)(2,1)S(1)} fusion(f32[4,8,128,128,6]{3,2,4,1,0:T(8,128)} %get-tuple-element.42, f32[128,4,6]{0,2,1:T(8,128)S(1)} %get-tuple-element.41, pred[8]{0:T(512)(128)(4,1)S(1)} %get-tuple-element.52, bf16[8,128,4,128]{1,3,2,0:T(8,128)(2,1)S(1)} %copy-done.9, f32[128,4,6]{0,2,1:T(8,128)S(1)} %get-tuple-element.9), kind=kOutput, calls=%fused_computation.51 | convolution fusion | flops 818675712 | bytes 14442504 | tf_op jit(solution)/shard_map/qgrpk,pkgd->qgrd/dot_general | solution.py:39
  257.9 0.0 copy-start.7
  257.9 2.5 fusion.10
  260.5 3.3 %fusion.26 = bf16[128,4,6,128]{0,3,2,1:T(8,128)(2,1)S(1)} fusion(f32[4,8,128,128,6]{3,2,4,1,0:T(8,128)S(1)} %get-tuple-element.43, f32[128,4,6]{0,2,1:T(8,128)S(1)} %get-tuple-element.10, pred[8]{0:T(512)(128)(4,1)S(1)} %get-tuple-element.52, bf16[8,128,4,128]{1,3,2,0:T(8,128)(2,1)S(1)} %copy-done.7, f32[128,4,6]{0,2,1:T(8,128)S(1)} %fusion.10), kind=kOutput, calls=%fused_computation.49 | convolution fusion | flops 818675712 | bytes 14442504 | tf_op jit(solution)/shard_map/qgrpk,pkgd->qgrd/dot_general | solution.py:39
  263.7 0.1 pad_maximum_fusion.4
  263.9 0.7 copy.55
  264.6 0.0 copy-start.4
  264.6 7.9 %bitcast_reduce_fusion.3 = (f32[128,4,6]{0,2,1:T(8,128)S(1)}, f32[4,8,128,128,6]{3,2,4,1,0:T(8,128)}) fusion(pred[8]{0:T(512)(128)(4,1)S(1)} %get-tuple-element.51, bf16[128,8,6,128]{0,3,2,1:T(8,128)(2,1)} %bitcast.212, bf16[8,128,4,128]{3,1,0,2:T(8,128)(2,1)} %copy.81), kind=kOutput, calls=%fused_computation.15 | convolution fusion | flops 814740480 | bytes 14430216 | tf_op jit(solution)/shard_map/qgrd,pkgd->qgrpk/dot_general | solution.py:30
  272.5 0.0 copy-done.2
  272.5 7.5 %fusion.4 = (f32[128,4,6]{0,2,1:T(8,128)S(1)}, f32[128,4,6]{0,2,1:T(8,128)S(1)}, f32[4,8,128,128,6]{3,2,4,1,0:T(8,128)S(1)}) fusion(f32[4,8,128,128,6]{3,2,4,1,0:T(8,128)} %get-tuple-element.45, f32[128,4,6]{0,2,1:T(8,128)S(1)} %get-tuple-element.44, pred[8]{0:T(512)(128)(4,1)S(1)} %get-tuple-element.51, bf16[128,8,6,128]{0,3,2,1:T(8,128)(2,1)S(1)} %bitcast.213, ...), kind=kOutput, calls=%fused_computation.21 | convolution fusion | flops 827320320 | bytes 27042304 | tf_op jit(solution)/shard_map/qgrd,pkgd->qgrpk/dot_general | solution.py:30
  280.0 7.6 %fusion.29 = bf16[128,4,6,128]{0,3,2,1:T(8,128)(2,1)S(1)} fusion(f32[4,8,128,128,6]{3,2,4,1,0:T(8,128)} %get-tuple-element.45, f32[128,4,6]{0,2,1:T(8,128)S(1)} %get-tuple-element.44, pred[8]{0:T(512)(128)(4,1)S(1)} %get-tuple-element.51, bf16[8,128,4,128]{1,3,2,0:T(8,128)(2,1)S(1)} %copy-done.8, f32[128,4,6]{0,2,1:T(8,128)S(1)} %get-tuple-element.6), kind=kOutput, calls=%fused_computation.55 | convolution fusion | flops 818675712 | bytes 14442504 | tf_op jit(solution)/shard_map/qgrpk,pkgd->qgrd/dot_general | solution.py:39
  287.7 2.5 fusion.6
  290.2 0.0 copy-done.6
  290.2 3.3 %fusion.28 = bf16[128,4,6,128]{0,3,2,1:T(8,128)(2,1)S(1)} fusion(f32[4,8,128,128,6]{3,2,4,1,0:T(8,128)S(1)} %get-tuple-element.46, f32[128,4,6]{0,2,1:T(8,128)S(1)} %get-tuple-element.8, pred[8]{0:T(512)(128)(4,1)S(1)} %get-tuple-element.51, bf16[8,128,4,128]{1,3,2,0:T(8,128)(2,1)S(1)} %copy-done.6, f32[128,4,6]{0,2,1:T(8,128)S(1)} %fusion.6), kind=kOutput, calls=%fused_computation.53 | convolution fusion | flops 818675712 | bytes 14442504 | tf_op jit(solution)/shard_map/qgrpk,pkgd->qgrd/dot_general | solution.py:39
  293.5 0.1 pad_maximum_fusion.3
  293.6 1.6 copy.54
  295.2 3.3 %pad_maximum_fusion = bf16[256,6144]{1,0:T(8,128)(2,1)} fusion(bf16[128,6144]{1,0:T(8,128)(2,1)S(1)} %copy.55, bf16[128,6144]{1,0:T(8,128)(2,1)} %copy.54), kind=kLoop, calls=%fused_computation.41 | loop fusion | flops 6291456 | bytes 6291456 | tf_op jit(solution)/shard_map/concatenate | solution.py:69
  (19 shorter events, 0.1 us)
Async XLA Ops:
  6.5 76.7 %all-gather.5.cloned.1.call-start = ((), (), s32[]{:S(2)}) async-start(), calls=%async_computation.2 | async-start | bytes 8912896 | tf_op jit(solution)/shard_map/all_gather | solution.py:55
  25.1 154.0 %all-gather.3.cloned.1.call-start = ((), (), s32[]{:S(2)}) async-start(), calls=%async_computation.1 | async-start | bytes 17825792 | tf_op jit(solution)/shard_map/all_gather | solution.py:54
  27.9 3.2 %copy-start.11 = (s32[2,5]{1,0:T(2,128)S(1)}, s32[2,5]{1,0:T(2,128)}, u32[]{:S(2)}) copy-start(s32[2,5]{1,0:T(2,128)} %param.11) | copy-start | bytes 124
  27.9 3.2 %copy-start.10 = (s32[2,3]{1,0:T(2,128)S(1)}, s32[2,3]{1,0:T(2,128)}, u32[]{:S(2)}) copy-start(s32[2,3]{1,0:T(2,128)} %param.12) | copy-start | bytes 76
  195.3 3.2 %copy-start = (bf16[3,128,2048]{2,1,0:T(8,128)(2,1)S(1)}, bf16[3,128,2048]{2,1,0:T(8,128)(2,1)}, u32[]{:S(2)}) copy-start(bf16[3,128,2048]{2,1,0:T(8,128)(2,1)} %get-tuple-element.49) | copy-start | bytes 4718596
  230.3 6.2 %copy-start.1 = (bf16[8,128,4,128]{3,1,0,2:T(8,128)(2,1)S(1)}, bf16[8,128,4,128]{3,1,0,2:T(8,128)(2,1)}, u32[]{:S(2)}) copy-start(bf16[8,128,4,128]{3,1,0,2:T(8,128)(2,1)} %copy.88) | copy-start | bytes 3145732
  231.8 4.7 %copy-start.3 = (bf16[128,6144]{0,1:T(8,128)(2,1)S(1)}, bf16[128,6144]{0,1:T(8,128)(2,1)}, u32[]{:S(2)}) copy-start(bf16[128,6144]{0,1:T(8,128)(2,1)} %copy.89) | copy-start | bytes 4718596
  236.5 6.3 %copy-start.5 = (bf16[8,128,4,128]{3,1,0,2:T(8,128)(2,1)S(1)}, bf16[8,128,4,128]{3,1,0,2:T(8,128)(2,1)}, u32[]{:S(2)}) copy-start(bf16[8,128,4,128]{3,1,0,2:T(8,128)(2,1)} %copy.92) | copy-start | bytes 3145732
  242.8 7.5 %copy-start.9 = (bf16[8,128,4,128]{1,3,2,0:T(8,128)(2,1)S(1)}, bf16[8,128,4,128]{1,3,2,0:T(8,128)(2,1)}, u32[]{:S(2)}) copy-start(bf16[8,128,4,128]{1,3,2,0:T(8,128)(2,1)} %get-tuple-element.29) | copy-start | bytes 3145732
  257.9 2.5 copy-start.7
  264.6 7.9 %copy-start.2 = (bf16[128,6144]{0,1:T(8,128)(2,1)S(1)}, bf16[128,6144]{0,1:T(8,128)(2,1)}, u32[]{:S(2)}) copy-start(bf16[128,6144]{0,1:T(8,128)(2,1)} %copy.82) | copy-start | bytes 4718596
  264.6 7.9 %copy-start.4 = (bf16[8,128,4,128]{3,1,0,2:T(8,128)(2,1)S(1)}, bf16[8,128,4,128]{3,1,0,2:T(8,128)(2,1)}, u32[]{:S(2)}) copy-start(bf16[8,128,4,128]{3,1,0,2:T(8,128)(2,1)} %copy.85) | copy-start | bytes 3145732
  272.5 7.5 %copy-start.8 = (bf16[8,128,4,128]{1,3,2,0:T(8,128)(2,1)S(1)}, bf16[8,128,4,128]{1,3,2,0:T(8,128)(2,1)}, u32[]{:S(2)}) copy-start(bf16[8,128,4,128]{1,3,2,0:T(8,128)(2,1)} %get-tuple-element.25) | copy-start | bytes 3145732
  287.7 2.5 copy-start.6
Sparse Core Ops, SparseCore 0:
  25.2 58.0 all-gather.4
  85.1 93.8 all-gather.2
where the time goes:
time: 308 us; the launch traced here: 305 us
  waiting for transfers between devices  138 us (45%)
  local copies, waits for them, and re-layouts  66 us (21%)
  matrix products  51 us (17%)
  other arithmetic  21.1 us (7%)
  blocking collectives  15.2 us (5%)
  between operations  13.7 us (4%)
    all_gather x1, waiting for transfers between devices, shards(): group_pool = lax.all_gather(keys_values, 'member', axis=1, tiled=True)  85.7 us
    all_gather x1, waiting for transfers between devices, shards(): cast_pool = lax.all_gather(arrived, 'member', axis=1, tiled=True)  51.9 us
    dot_general x4, matrix products, attend_rows(): jnp.einsum('qgrd,pkgd->qgrpk', query_part, keys_part, preferred_element_t...  29.2 us
    dot_general x4, matrix products, attend_rows(): jnp.einsum('qgrpk,pkgd->qgrd', rounded, values_part, preferred_element_ty...  21.8 us
    gather x2, local copies, waits for them, and re-layouts, shards(): jnp.take(group_pool, jnp.maximum(local_row, 0), axis=0)  16.3 us
    all_to_all x1, blocking collectives, shards(): lax.all_to_all(outgoing, 'group', split_axis=0, concat_axis=0, tiled=True)  15.2 us
    unnamed x30, local copies, waits for them, and re-layouts  12.5 us
    gather x2, local copies, waits for them, and re-layouts, shards(): jnp.take(cast_pool, jnp.maximum(remote_row, 0), axis=0)  8.06 us
  transfers between devices with their start and end apart: 2, of which 2 were waited for; matrix products, arithmetic and copies ran while one was open for 5% of the time, Pallas kernels for 0%

commit v1 on v0

v1 whole, which is shorter than its diff:
```python
import functools

import jax
import jax.numpy as jnp
from jax import lax
from jax.experimental import pallas as pl
from jax.experimental.pallas import tpu as pltpu
from jax.sharding import PartitionSpec as P

HEADS, KV_HEADS, HEAD_DIM = 48, 8, 128
CH = 6
REPEAT = HEADS // KV_HEADS
SCALE = HEAD_DIM ** -0.5 * 1.4426950408889634


def attend_kernel(local_ref, remote_ref, table_ref, q_ref, pool_a, pool_b, out_ref, kv, stacked, scores, weights, sems):
    block, head = pl.program_id(0), pl.program_id(1)
    n_local, n_remote = local_ref.shape[1], remote_ref.shape[1]
    rows = q_ref.shape[0]
    keys = kv.shape[1] // (n_local + n_remote)
    members = keys // 8

    def counts(b):
        near = sum((local_ref[b, i] >= 0).astype(jnp.int32) for i in range(n_local))
        far = sum((remote_ref[b, i] >= 0).astype(jnp.int32) for i in range(n_remote))
        return near, far

    near, far = counts(block)
    total = near + far
    pairs = lax.div(total + 1, 2)

    def copy(b, pool, unit, slot, m):
        return pltpu.make_async_copy(
            pool.at[unit], kv.at[b, pl.ds(pl.multiple_of(slot * keys + m * 8, 8), 8), :], sems.at[b])

    def fetch(b):
        near, far = counts(b)

        def local_slot(s, _):
            which = local_ref[b, s]
            for m in range(members):
                copy(b, pool_a, table_ref[which * members + m], s, m).start()
            return 0

        def remote_slot(s, _):
            which = remote_ref[b, s] + 32
            for m in range(members):
                copy(b, pool_b, table_ref[which * members + m], near + s, m).start()
            return 0

        lax.fori_loop(0, near, local_slot, 0)
        lax.fori_loop(0, far, remote_slot, 0)

        @pl.when(lax.rem(near + far, 2) == 1)
        def _():
            which = local_ref[b, 0]
            for m in range(members):
                copy(b, pool_a, table_ref[which * members + m], near + far, m).start()

    @pl.when(jnp.logical_and(block == 0, head == 0))
    def _():
        for b in range(2):
            fetch(b)

    @pl.when(head == 0)
    def _():
        def drain(s, _):
            pltpu.make_async_copy(
                kv.at[block, pl.ds(0, 2 * keys), :], kv.at[block, pl.ds(0, 2 * keys), :], sems.at[block]).wait()
            return 0
        lax.fori_loop(0, pairs, drain, 0)

    kcol = pl.multiple_of(head * HEAD_DIM, HEAD_DIM)
    vcol = pl.multiple_of(KV_HEADS * HEAD_DIM + head * HEAD_DIM, HEAD_DIM)
    def work(pairs):
        for r in range(REPEAT):
            stacked[r * rows:(r + 1) * rows, :] = q_ref[:, r * HEAD_DIM:(r + 1) * HEAD_DIM]
        bias = jnp.where(2 * pairs == total, 0.0, -jnp.inf)
        q = stacked[...]
        for j in range(pairs):
            k = kv[block, j * 2 * keys:(j + 1) * 2 * keys, pl.ds(kcol, HEAD_DIM)]
            scores[j] = lax.dot_general(q, k, (((1,), (1,)), ((), ())), preferred_element_type=jnp.float32)
        for r in range(REPEAT):
            span = slice(r * rows, (r + 1) * rows)
            parts = []
            for j in range(pairs):
                parts.append(scores[j, span, :keys])
                last = scores[j, span, keys:]
                parts.append(last + bias if j == pairs - 1 else last)
            top = functools.reduce(jnp.maximum, parts)
            top = jnp.max(top, axis=1, keepdims=True) * SCALE
            for i, part in enumerate(parts):
                weights[span, i * keys:(i + 1) * keys] = jnp.exp2(part * SCALE - top).astype(jnp.bfloat16)
        v = kv[block, :pairs * 2 * keys, pl.ds(vcol, HEAD_DIM)]
        both = jnp.concatenate([v, jnp.ones((pairs * 2 * keys, HEAD_DIM), jnp.bfloat16)], axis=1)
        for r in range(0, REPEAT, CH):
            acc = jnp.dot(weights[r * rows:(r + CH) * rows, :pairs * 2 * keys], both, preferred_element_type=jnp.float32)
            out = (acc[:, :HEAD_DIM] / acc[:, HEAD_DIM:]).astype(jnp.bfloat16)
            for i in range(CH):
                out_ref[:, (r + i) * HEAD_DIM:(r + i + 1) * HEAD_DIM] = out[i * rows:(i + 1) * rows]

    for count in range(1, kv.shape[1] // (2 * keys) + 1):
        pl.when(pairs == count)(functools.partial(work, count))


def attend(local_lists, remote_lists, table, queries, pool_a, pool_b):
    blocks = local_lists.shape[0]
    rows = queries.shape[0] // blocks
    slots = local_lists.shape[1] + remote_lists.shape[1]
    keys = 128
    width = REPEAT * HEAD_DIM
    return pl.pallas_call(
        attend_kernel,
        out_shape=jax.ShapeDtypeStruct(queries.shape, jnp.bfloat16),
        grid_spec=pltpu.PrefetchScalarGridSpec(
            num_scalar_prefetch=3, grid=(blocks, KV_HEADS),
            in_specs=[pl.BlockSpec((rows, width), lambda b, h, *_: (b, h)),
                      pl.BlockSpec(memory_space=pl.ANY), pl.BlockSpec(memory_space=pl.ANY)],
            out_specs=pl.BlockSpec((rows, width), lambda b, h, *_: (b, h)),
            scratch_shapes=[
                pltpu.VMEM((blocks, slots * keys, 2 * KV_HEADS * HEAD_DIM), jnp.bfloat16),
                pltpu.VMEM((REPEAT * rows, HEAD_DIM), jnp.bfloat16),
                pltpu.VMEM((slots // 2, REPEAT * rows, 2 * keys), jnp.float32),
                pltpu.VMEM((REPEAT * rows, slots * keys), jnp.bfloat16),
                pltpu.SemaphoreType.DMA((blocks,)),
            ]),
        compiler_params=pltpu.CompilerParams(vmem_limit_bytes=56 << 20),
        name="attend",
    )(local_lists, remote_lists, table, queries, pool_a, pool_b)


def shards(queries, keys_values, local_lists, remote_lists, send_blocks):
    outgoing = jnp.take(keys_values, send_blocks[0], axis=0)
    arrived = lax.all_to_all(outgoing, "group", split_axis=0, concat_axis=0, tiled=True)
    near = lax.all_gather(keys_values, "member", axis=0, tiled=True)
    far = lax.all_gather(arrived, "member", axis=0, tiled=True)
    blocks, slabs = keys_values.shape[0], arrived.shape[0]
    members = near.shape[0] // blocks
    order = jnp.arange(members, dtype=jnp.int32)
    table = jnp.concatenate([
        (jnp.arange(blocks, dtype=jnp.int32)[:, None] + order * blocks).reshape(-1),
        (jnp.arange(slabs, dtype=jnp.int32)[:, None] + order * slabs).reshape(-1)])
    return attend(local_lists, remote_lists, table, queries, near, far)


def solution(mesh):
    placed = (
        P(("group", "member"), None),
        P("group", "member", None),
        P(("group", "member"), None),
        P(("group", "member"), None),
        P("group", None),
    )
    return jax.shard_map(
        shards, mesh=mesh, in_specs=placed, out_specs=P(("group", "member"), None), check_vma=False
    )
```

time: 308 us -> 217 us (0.70); the launches traced: 305 us -> 218 us
  local copies, waits for them, and re-layouts: 66 us -> 1.97 us
  matrix products: 51 us -> 0 us
  Pallas kernels: 0 us -> 31.7 us
  other arithmetic: 21.1 us -> 2.06 us
  waiting for transfers between devices: 138 us -> 153 us
    dot_general x8 -> x0, matrix products: 51 us -> none  [the longest x4 29.2 us: attend_rows(): jnp.einsum('qgrd,pkgd->qgrpk', query_part, keys_part, preferred_element_t...]
    pallas_call x0 -> x1, Pallas kernels: none -> 31.7 us  [attend(): pl.pallas_call(attend_kernel, out_shape=jax.ShapeDtypeStruct(queries.shap...]
    slice x9 -> x0, local copies, waits for them, and re-layouts: 25.1 us -> none  [the longest x2 6.93 us: attend_rows(): listed[:, :, :key_width]]
    gather x5 -> x1, local copies, waits for them, and re-layouts: 26.1 us -> 1.81 us  [shards(): outgoing = jnp.take(keys_values, send_blocks[0], axis=0)]
    all_gather x2, waiting for transfers between devices: 138 us -> 152 us  [the longest x1 95.8 us: shards(): near = lax.all_gather(keys_values, 'member', axis=0, tiled=True)]
    unnamed x30 -> x0, local copies, waits for them, and re-layouts: 12.5 us -> none
    concatenate x6 -> x1, other arithmetic: 9.36 us -> 0.6 us  [shards(): jnp.concatenate([(jnp.arange(blocks, dtype=jnp.int32)[:, None] + order *...]
    select_n x4 -> x2, other arithmetic: 5.94 us -> 0.77 us  [shards(): outgoing = jnp.take(keys_values, send_blocks[0], axis=0)]
  transfers between devices with their start and end apart: 2 -> 2, of which waited for: 2 -> 2; matrix products, arithmetic and copies ran while one was open for 5% -> 0% of each run, Pallas kernels for 0% -> 0%
where the time goes in v1:
time: 217 us; the launch traced here: 218 us
  waiting for transfers between devices  153 us (71%)
  Pallas kernels  31.7 us (15%)
  blocking collectives  15.2 us (7%)
  between operations  13.5 us (6%)
    all_gather x1, waiting for transfers between devices, shards(): near = lax.all_gather(keys_values, 'member', axis=0, tiled=True)  95.8 us
    all_gather x1, waiting for transfers between devices, shards(): far = lax.all_gather(arrived, 'member', axis=0, tiled=True)  56.6 us
    pallas_call x1, Pallas kernels, attend(): pl.pallas_call(attend_kernel, out_shape=jax.ShapeDtypeStruct(queries.shap...  31.7 us
    all_to_all x1, blocking collectives, shards(): lax.all_to_all(outgoing, 'group', split_axis=0, concat_axis=0, tiled=True)  15.2 us
  transfers between devices with their start and end apart: 2, of which 2 were waited for; matrix products, arithmetic and copies ran while one was open for 0% of the time, Pallas kernels for 0%

profile of v1, /device:TPU:14, one launch (start us, length us, event | category | flops | bytes accessed | tf_op | source)
XLA Modules:
  0.0 217.5 jit_solution(993446159727157013)
XLA Ops:
  6.5 0.0 all-gather.5.cloned.1.call-start
  6.5 0.7 fusion
  7.2 0.7 compare_and_fusion
  7.9 1.8 gather_fusion
  9.7 0.1 broadcast_select_fusion
  9.8 15.2 %all_to_all.5 = bf16[16,8,2048]{2,1,0:T(8,128)(2,1)} all-to-all(bf16[16,8,2048]{2,1,0:T(8,128)(2,1)S(1)} %broadcast_select_fusion), channel_id=1, replica_groups=mesh['group'=16,'member'=16] {'group'}, dimensions={0} | all-to-all | bytes 1048576 | tf_op jit(solution)/shard_map/all_to_all | solution.py:134
  25.0 0.0 all-gather.5.cloned.1.call-update
  25.1 0.0 all-gather.3.cloned.1.call-start
  25.1 0.7 all-gather.3.cloned.1.call-update
  25.8 0.1 add.56
  25.9 0.1 add.52
  26.0 0.6 pad_add_fusion.table_ref
  26.6 56.6 %all-gather.5.cloned.1.call-done.pool_b = bf16[256,8,2048]{2,1,0:T(8,128)(2,1)} async-done(((bf16[16,8,2048]{2,1,0:T(8,128)(2,1)}), bf16[256,8,2048]{2,1,0:T(8,128)(2,1)}) %all-gather.5.cloned.1.call-update) | async-done | bytes 8388624 | tf_op jit(solution)/shard_map/all_gather | solution.py:136
  83.2 95.8 %all-gather.3.cloned.1.call-done.pool_a = bf16[512,8,2048]{2,1,0:T(8,128)(2,1)} async-done(((bf16[32,8,2048]{2,1,0:T(8,128)(2,1)}), bf16[512,8,2048]{2,1,0:T(8,128)(2,1)}) %all-gather.3.cloned.1.call-update) | async-done | bytes 16777232 | tf_op jit(solution)/shard_map/all_gather | solution.py:135
  179.0 31.7 %attend.1 = bf16[256,6144]{1,0:T(8,128)(2,1)} custom-call(s32[2,5]{1,0:T(2,128)} %local_ref.1, s32[2,3]{1,0:T(2,128)} %remote_ref.1, s32[768]{0:T(1024)} %pad_add_fusion.table_ref, bf16[256,6144]{1,0:T(8,128)(2,1)} %q_ref.1, bf16[512,8,2048]{2,1,0:T(8,128)(2,1)} %all-gather.3.cloned.1.call-done.pool_a, bf16[256,8,2048]{2,1,0:T(8,128)(2,1)} %all-gather.5.cloned.1.call-done.pool_b), custom_call_target="tpu_custom_call" | custom-call | tf_op jit(solution)/shard_map/attend/pallas_call | solution.py:112
  (5 shorter events, 0.0 us)
Async XLA Ops:
  6.5 76.7 %all-gather.5.cloned.1.call-start = ((), (), s32[]{:S(2)}) async-start(), calls=%async_computation.2 | async-start | bytes 8912896 | tf_op jit(solution)/shard_map/all_gather | solution.py:136
  25.1 153.9 %all-gather.3.cloned.1.call-start = ((), (), s32[]{:S(2)}) async-start(), calls=%async_computation.1 | async-start | bytes 17825792 | tf_op jit(solution)/shard_map/all_gather | solution.py:135
Sparse Core Ops, SparseCore 0:
  25.2 58.0 all-gather.4
  85.1 93.8 all-gather.2
